TPU v7x, 512 devices: a whole 4x8x8 slice. The times are simulated.
512 devices in a mesh: seq: 64 (over z_hi, y, core), grp: 8 (over x, z_lo).
Axes of the slice: x: 4, y: 8, z: 8 (z_hi: 4, z_lo: 2; z = z_hi * 2 + z_lo), core: 2. Of those that a mesh axis runs over, the one named last changes fastest.
Arguments:
- embeddings: bfloat16 [1536, 32768], P('grp', 'seq'), may hold values from -6 to 6
- hilbert_order: int32 [32768], P('seq'), may hold values from 0 to 32767, as said below
- cotangent: bfloat16 [1536, 32768], P('grp', 'seq'), may hold values from -6 to 6
- first_conv_weight: bfloat16 [8, 110592], P('grp'), may hold values from -0.25 to 0.25
- first_pointwise_weight: bfloat16 [1536, 1536], P('grp'), may hold values from -0.21875 to 0.21875
- second_conv_weight: bfloat16 [8, 110592], P('grp'), may hold values from -0.25 to 0.25
- second_pointwise_weight: bfloat16 [1536, 1536], P('grp'), may hold values from -0.21875 to 0.21875
Outputs:
- emb_grad: bfloat16 [1536, 32768], P('grp', 'seq')
- first_conv_gradient: bfloat16 [8, 110592], P('grp')
- first_pointwise_gradient: bfloat16 [1536, 1536], P('grp')
- second_conv_gradient: bfloat16 [8, 110592], P('grp')
- second_pointwise_gradient: bfloat16 [1536, 1536], P('grp')
Inputs may be any that keep to these rules, and one draw needn't show every extreme that they name: `hilbert_order`: every aligned block of 512 positions holds each patch index of that same block exactly once.
All inputs are finite; a program needn't handle non-finite values.
Results may differ from a plain program's by a relative error of at most 0.018.
Values may be sent and summed in bfloat16 or wider, within the bound.
No kernel may reach another device: no remote copies, remote signals or barrier semaphores. Data moves between devices by JAX's collectives and lax.ppermute only.
A program may use at most 64 MiB of HBM per device.

v0:
```python
import jax
import jax.numpy as jnp
from jax import lax
from jax.sharding import PartitionSpec as P

CG = 192


def passed_along(block, axis, distance):
    devices = range(lax.axis_size(axis))
    route = [(i - distance, i) for i in devices if i - distance in devices]
    return lax.ppermute(block, axis, route)


def shard_taps(inputs, shift_by):
    earlier = passed_along(inputs, "seq", shift_by)
    following = passed_along(inputs, "seq", -shift_by)
    return (earlier, inputs, following)


def grad_taps(grad_pre, shift_by):
    following = passed_along(grad_pre, "seq", -shift_by)
    earlier = passed_along(grad_pre, "seq", shift_by)
    return (following, grad_pre, earlier)


def tap_weights(conv_weight, tap):
    groups_here = conv_weight.shape[0]
    return conv_weight.reshape(groups_here, 3, CG, CG)[:, tap]


def group_apply(values, weight_tap):
    channels, col_count = values.shape
    groups_here = channels // CG
    return jnp.einsum(
        "git,gio->got",
        values.reshape(groups_here, CG, col_count),
        weight_tap,
        preferred_element_type=jnp.float32,
    ).reshape(channels, col_count)


def group_back(grads, weight_tap):
    channels, col_count = grads.shape
    groups_here = channels // CG
    return jnp.einsum(
        "got,gio->git",
        grads.reshape(groups_here, CG, col_count),
        weight_tap,
        preferred_element_type=jnp.float32,
    ).reshape(channels, col_count)


def group_grad(values, grads):
    channels, col_count = values.shape
    groups_here = channels // CG
    return jnp.einsum(
        "git,got->gio",
        values.reshape(groups_here, CG, col_count),
        grads.reshape(groups_here, CG, col_count),
        preferred_element_type=jnp.float32,
    )


def block_forward_step(inputs, conv_weight, shift_by):
    tap_set = shard_taps(inputs, shift_by)
    hidden = (
        group_apply(tap_set[0], tap_weights(conv_weight, 0))
        + group_apply(tap_set[1], tap_weights(conv_weight, 1))
        + group_apply(tap_set[2], tap_weights(conv_weight, 2))
    )
    activated = jax.nn.silu(hidden).astype(jnp.bfloat16)
    gathered = lax.all_gather(activated, "grp", axis=0, tiled=True)
    return (tap_set, hidden, gathered)


def block_backward_step(
    grad_out, tap_set, hidden, gathered, conv_weight, pointwise, shift_by, gradient_scale
):
    shard_width, col_count = grad_out.shape
    groups_here = conv_weight.shape[0]
    point_grad = lax.dot_general(
        grad_out, gathered, (((1,), (1,)), ((), ())), preferred_element_type=jnp.float32
    )
    weight_rows = lax.all_to_all(pointwise, "grp", split_axis=1, concat_axis=0, tiled=True)
    block_in = lax.all_gather(grad_out, "grp", axis=0, tiled=True)
    width_in = block_in.shape[0]
    shard_count = width_in // shard_width
    partials = jnp.einsum(
        "jot,joi->jit",
        block_in.reshape(shard_count, shard_width, col_count),
        weight_rows.reshape(shard_count, shard_width, shard_width),
        preferred_element_type=jnp.float32,
    )
    rounded = lax.optimization_barrier(partials.astype(jnp.bfloat16))
    grad_hidden = jnp.sum(rounded.astype(jnp.float32), axis=0)
    sigmoid_h = jax.nn.sigmoid(hidden)
    grad_pre = (grad_hidden * sigmoid_h * (1.0 + hidden * (1.0 - sigmoid_h))).astype(jnp.bfloat16)
    conv_grad = jnp.stack(
        [group_grad(tap_values, grad_pre) for tap_values in tap_set], axis=1
    ).reshape(groups_here, 3 * CG * CG)
    moved = grad_taps(grad_pre, shift_by)
    grad_input = (
        grad_out.astype(jnp.float32)
        + group_back(moved[0], tap_weights(conv_weight, 0))
        + group_back(moved[1], tap_weights(conv_weight, 1))
        + group_back(moved[2], tap_weights(conv_weight, 2))
    )
    summed = lax.psum((conv_grad, point_grad), "seq")
    conv_result = (summed[0] * gradient_scale).astype(jnp.bfloat16)
    point_result = (summed[1] * gradient_scale).astype(jnp.bfloat16)
    return (grad_input.astype(jnp.bfloat16), conv_result, point_result)


def local(
    embeddings,
    hilbert_order,
    cotangent,
    first_conv_weight,
    first_pointwise_weight,
    second_conv_weight,
    second_pointwise_weight,
):
    seq_count = lax.axis_size("seq")
    gradient_scale = float(embeddings.shape[1] * seq_count) ** (-0.5)
    near_shift = seq_count // 16
    far_shift = seq_count // 8
    local_index = hilbert_order - lax.axis_index("seq") * hilbert_order.shape[0]
    initial_token_rows = jnp.take(embeddings, local_index, axis=1)
    first_tap_rows, first_hidden_state, near_full = block_forward_step(
        initial_token_rows, first_conv_weight, near_shift
    )
    middle_rows = (
        initial_token_rows.astype(jnp.float32)
        + jnp.dot(first_pointwise_weight, near_full, preferred_element_type=jnp.float32)
    ).astype(jnp.bfloat16)
    second_tap_rows, second_hidden_state, far_full = block_forward_step(
        middle_rows, second_conv_weight, far_shift
    )
    middle_gradient, second_conv_gradient, second_pointwise_gradient = block_backward_step(
        cotangent,
        second_tap_rows,
        second_hidden_state,
        far_full,
        second_conv_weight,
        second_pointwise_weight,
        far_shift,
        gradient_scale,
    )
    start_gradient, first_conv_gradient, first_pointwise_gradient = block_backward_step(
        middle_gradient,
        first_tap_rows,
        first_hidden_state,
        near_full,
        first_conv_weight,
        first_pointwise_weight,
        near_shift,
        gradient_scale,
    )
    emb_grad = jnp.zeros_like(start_gradient).at[:, local_index].set(start_gradient)
    return (
        emb_grad,
        first_conv_gradient,
        first_pointwise_gradient,
        second_conv_gradient,
        second_pointwise_gradient,
    )


def solution(mesh):
    placed = (
        P("grp", "seq"),
        P("seq"),
        P("grp", "seq"),
        P("grp", None),
        P("grp", None),
        P("grp", None),
        P("grp", None),
    )
    return jax.shard_map(
        local,
        mesh=mesh,
        in_specs=placed,
        out_specs=(P("grp", "seq"), P("grp", None), P("grp", None), P("grp", None), P("grp", None)),
        check_vma=False,
    )
```

profile of v0, /device:TPU:1, one launch (start us, length us, event | category | flops | bytes accessed | tf_op | source)
XLA Modules:
  0.0 842.4 jit_solution(17735297071518127190)
XLA Ops:
  9.8 2.0 gather_fusion
  13.2 5.7 collective-permute-start
  20.7 1.6 collective-permute-done.1
  24.8 9.1 %all-to-all-start = ((bf16[192,8,192]{0,2,1:T(8,128)(2,1)}), bf16[192,8,192]{0,2,1:T(8,128)(2,1)S(1)}, u32[]{:S(2)}, u32[]{:S(2)}) async-start(bf16[192,8,192]{0,2,1:T(8,128)(2,1)} %bitcast), calls=%async_computation | async-start | bytes 1572864 | tf_op jit(solution)/shard_map/all_to_all | solution.py:85
  35.5 15.1 %all-to-all-done = bf16[192,8,192]{0,2,1:T(8,128)(2,1)S(1)} async-done(((bf16[192,8,192]{0,2,1:T(8,128)(2,1)}), bf16[192,8,192]{0,2,1:T(8,128)(2,1)S(1)}, u32[]{:S(2)}, u32[]{:S(2)}) %all-to-all-start) | async-done | bytes 589856 | tf_op jit(solution)/shard_map/all_to_all | solution.py:85
  50.7 21.0 %all-gather.5.cloned.1.call-done = bf16[1536,512]{1,0:T(8,128)(2,1)} async-done(((bf16[192,512]{1,0:T(8,128)(2,1)}), bf16[1536,512]{1,0:T(8,128)(2,1)}) %all-gather.5.cloned.1.call-update) | async-done | bytes 1572880 | tf_op jit(solution)/shard_map/all_gather | solution.py:86
  71.6 2.0 convolution_convert_fusion.1
  73.9 49.9 %all-gather.7.cloned.1.call-done = bf16[1536,512]{1,0:T(8,128)(2,1)} async-done(((bf16[192,512]{1,0:T(8,128)(2,1)}), bf16[1536,512]{1,0:T(8,128)(2,1)}) %all-gather.7.cloned.1.call-update) | async-done | bytes 1572880 | tf_op jit(solution)/shard_map/all_gather | solution.py:73
  123.7 1.9 fusion.12
  126.9 7.9 collective-permute-start.2
  139.9 15.3 %collective-permute-start.5 = (bf16[192,512]{1,0:T(8,128)(2,1)S(1)}, bf16[192,512]{1,0:T(8,128)(2,1)S(1)}, u32[]{:S(2)}, u32[]{:S(2)}) collective-permute-start(bf16[192,512]{1,0:T(8,128)(2,1)S(1)} %get-tuple-element.17), channel_id=1, source_target_pairs={{0,64},{8,72},{16,80},{24,88},{32,96},{40,104},{48,112},{56,120},{... | collective-permute-start | bytes 589832 | tf_op jit(solution)/shard_map/ppermute | solution.py:12
  156.6 3.6 collective-permute-done.5
  162.3 3.7 all-to-all-start.1
  168.1 1.7 fusion.27
  169.9 39.5 %all-gather.11.cloned.1.call-done = bf16[1536,512]{1,0:T(8,128)(2,1)} async-done(((bf16[192,512]{1,0:T(8,128)(2,1)}), bf16[1536,512]{1,0:T(8,128)(2,1)}) %all-gather.11.cloned.1.call-update) | async-done | bytes 1572880 | tf_op jit(solution)/shard_map/all_gather | solution.py:73
  209.4 3.1 convolution_bitcast_fusion
  212.5 49.4 %all-gather.9.cloned.1.call-done = bf16[1536,512]{1,0:T(8,128)(2,1)} async-done(((bf16[192,512]{1,0:T(8,128)(2,1)}), bf16[1536,512]{1,0:T(8,128)(2,1)}) %all-gather.9.cloned.1.call-update) | async-done | bytes 1572880 | tf_op jit(solution)/shard_map/all_gather | solution.py:86
  261.9 2.0 fusion
  267.1 4.2 collective-permute-start.7
  273.0 13.5 %collective-permute-done.6 = bf16[192,512]{1,0:T(8,128)(2,1)S(1)} collective-permute-done((bf16[192,512]{1,0:T(8,128)(2,1)S(1)}, bf16[192,512]{1,0:T(8,128)(2,1)S(1)}, u32[]{:S(2)}, u32[]{:S(2)}) %collective-permute-start.6) | collective-permute-done | bytes 196640 | tf_op jit(solution)/shard_map/ppermute | solution.py:12
  287.0 2.4 scatter_custom_fusion
  290.2 540.1 %all-reduce.3.cloned.1.call-done = (f32[1,110592]{1,0:T(1,128)}, f32[192,1536]{1,0:T(8,128)}, f32[1,110592]{1,0:T(1,128)}, f32[192,1536]{1,0:T(8,128)}) async-done(((f32[1,110592]{1,0:T(1,128)}, f32[192,1536]{1,0:T(8,128)}, f32[1,110592]{1,0:T(1,128)}, f32[192,1536]{1,0:T(8,128)}), (f32[1,110592]{1,0:T(1,128)}, f32[192,1536]{1,0:T(8,128)}, f32[1,110592]{1,0:T(1,128)}, ...) | async-done | bytes 3244048 | tf_op jit(solution)/shard_map/psum | solution.py:109
  830.3 3.1 multiply_convert_fusion.2
  833.3 2.5 multiply_convert_fusion
  (98 shorter events, 28.1 us)
Async XLA Ops:
  7.2 64.5 %all-gather.5.cloned.1.call-start = ((), (), s32[]{:S(2)}) async-start(), calls=%async_computation.2 | async-start | bytes 1769472 | tf_op jit(solution)/shard_map/all_gather | solution.py:86
  7.9 11.0 %copy-start.13 = (bf16[1,110592]{1,0:T(2,128)(2,1)S(1)}, bf16[1,110592]{1,0:T(2,128)(2,1)}, u32[]{:S(2)}) copy-start(bf16[1,110592]{1,0:T(2,128)(2,1)} %param.10) | copy-start | bytes 663556
  7.9 115.8 %all-gather.7.cloned.1.call-start = ((), (), s32[]{:S(2)}) async-start(), calls=%async_computation.3 | async-start | bytes 1769472 | tf_op jit(solution)/shard_map/all_gather | solution.py:73
  11.9 10.4 %collective-permute-start.1 = (bf16[192,512]{1,0:T(8,128)(2,1)S(1)}, bf16[192,512]{1,0:T(8,128)(2,1)S(1)}, u32[]{:S(2)}, u32[]{:S(2)}) collective-permute-start(bf16[192,512]{1,0:T(8,128)(2,1)S(1)} %fusion.17), channel_id=1, source_target_pairs={{32,0},{40,8},{48,16},{56,24},{64,32},{72,40},{80,48},{88,56},{96,... | collective-permute-start | bytes 589832 | tf_op jit(solution)/shard_map/ppermute | solution.py:12
  13.2 9.3 %collective-permute-start = (bf16[192,512]{1,0:T(8,128)(2,1)S(1)}, bf16[192,512]{1,0:T(8,128)(2,1)S(1)}, u32[]{:S(2)}, u32[]{:S(2)}) collective-permute-start(bf16[192,512]{1,0:T(8,128)(2,1)S(1)} %fusion.17), channel_id=1, source_target_pairs={{0,32},{8,40},{16,48},{24,56},{32,64},{40,72},{48,80},{56,88},{64,... | collective-permute-start | bytes 589832 | tf_op jit(solution)/shard_map/ppermute | solution.py:12
  20.4 3.3 copy-start.3
  23.7 10.3 %copy-start.14 = (bf16[1,110592]{1,0:T(2,128)(2,1)S(1)}, bf16[1,110592]{1,0:T(2,128)(2,1)}, u32[]{:S(2)}) copy-start(bf16[1,110592]{1,0:T(2,128)(2,1)} %param.12) | copy-start | bytes 663556
  24.8 25.8 %all-to-all-start = ((bf16[192,8,192]{0,2,1:T(8,128)(2,1)}), bf16[192,8,192]{0,2,1:T(8,128)(2,1)S(1)}, u32[]{:S(2)}, u32[]{:S(2)}) async-start(bf16[192,8,192]{0,2,1:T(8,128)(2,1)} %bitcast), calls=%async_computation | async-start | bytes 1572864 | tf_op jit(solution)/shard_map/all_to_all | solution.py:85
  33.9 175.5 %all-gather.11.cloned.1.call-start = ((), (), s32[]{:S(2)}) async-start(), calls=%async_computation.5 | async-start | bytes 1769472 | tf_op jit(solution)/shard_map/all_gather | solution.py:73
  73.6 50.1 %copy-start.2 = (bf16[192,1536]{1,0:T(8,128)(2,1)S(1)}, bf16[192,1536]{1,0:T(8,128)(2,1)}, u32[]{:S(2)}) copy-start(bf16[192,1536]{1,0:T(8,128)(2,1)} %param.11) | copy-start | bytes 1769476
  125.6 10.9 %collective-permute-start.3 = (bf16[192,512]{1,0:T(8,128)(2,1)S(1)}, bf16[192,512]{1,0:T(8,128)(2,1)S(1)}, u32[]{:S(2)}, u32[]{:S(2)}) collective-permute-start(bf16[192,512]{1,0:T(8,128)(2,1)S(1)} %fusion.12), channel_id=1, source_target_pairs={{64,0},{72,8},{80,16},{88,24},{96,32},{104,40},{112,48},{120,56},{... | collective-permute-start | bytes 589832 | tf_op jit(solution)/shard_map/ppermute | solution.py:12
  126.9 10.5 %collective-permute-start.2 = (bf16[192,512]{1,0:T(8,128)(2,1)S(1)}, bf16[192,512]{1,0:T(8,128)(2,1)S(1)}, u32[]{:S(2)}, u32[]{:S(2)}) collective-permute-start(bf16[192,512]{1,0:T(8,128)(2,1)S(1)} %fusion.12), channel_id=1, source_target_pairs={{0,64},{8,72},{16,80},{24,88},{32,96},{40,104},{48,112},{56,120},{... | collective-permute-start | bytes 589832 | tf_op jit(solution)/shard_map/ppermute | solution.py:12
  137.2 19.2 %copy-start.5 = (bf16[192,512]{1,0:T(8,128)(2,1)S(1)}, bf16[192,512]{1,0:T(8,128)(2,1)}, u32[]{:S(2)}) copy-start(bf16[192,512]{1,0:T(8,128)(2,1)} %param.9) | copy-start | bytes 589828
  138.5 123.3 %all-gather.9.cloned.1.call-start = ((), (), s32[]{:S(2)}) async-start(), calls=%async_computation.4 | async-start | bytes 1769472 | tf_op jit(solution)/shard_map/all_gather | solution.py:86
  138.6 17.8 %collective-permute-start.4 = (bf16[192,512]{1,0:T(8,128)(2,1)S(1)}, bf16[192,512]{1,0:T(8,128)(2,1)S(1)}, u32[]{:S(2)}, u32[]{:S(2)}) collective-permute-start(bf16[192,512]{1,0:T(8,128)(2,1)S(1)} %get-tuple-element.17), channel_id=1, source_target_pairs={{64,0},{72,8},{80,16},{88,24},{96,32},{104,40},{112,48},{120,56},{... | collective-permute-start | bytes 589832 | tf_op jit(solution)/shard_map/ppermute | solution.py:12
  139.9 20.3 %collective-permute-start.5 = (bf16[192,512]{1,0:T(8,128)(2,1)S(1)}, bf16[192,512]{1,0:T(8,128)(2,1)S(1)}, u32[]{:S(2)}, u32[]{:S(2)}) collective-permute-start(bf16[192,512]{1,0:T(8,128)(2,1)S(1)} %get-tuple-element.17), channel_id=1, source_target_pairs={{0,64},{8,72},{16,80},{24,88},{32,96},{40,104},{48,112},{56,120},{... | collective-permute-start | bytes 589832 | tf_op jit(solution)/shard_map/ppermute | solution.py:12
  162.3 4.0 copy-start.11
  162.3 4.2 copy-start.19
  162.3 50.2 %all-to-all-start.1 = ((bf16[192,8,192]{0,2,1:T(8,128)(2,1)}), bf16[192,8,192]{0,2,1:T(8,128)(2,1)S(1)}, u32[]{:S(2)}, u32[]{:S(2)}) async-start(bf16[192,8,192]{0,2,1:T(8,128)(2,1)} %bitcast.17), calls=%async_computation.1 | async-start | bytes 1572864 | tf_op jit(solution)/shard_map/all_to_all | solution.py:85
  166.0 664.3 %all-reduce.3.cloned.1.call-start = ((), (), s32[]{:S(2)}) async-start(), calls=%async_computation.6 | async-start | bytes 6488064 | tf_op jit(solution)/shard_map/psum | solution.py:109
  168.1 41.3 %copy-start.6 = (bf16[192,512]{1,0:T(8,128)(2,1)S(1)}, bf16[192,512]{1,0:T(8,128)(2,1)}, u32[]{:S(2)}) copy-start(bf16[192,512]{1,0:T(8,128)(2,1)} %param.9) | copy-start | bytes 589828
  267.1 5.7 copy-start.4
  267.1 19.5 %collective-permute-start.7 = (bf16[192,512]{1,0:T(8,128)(2,1)S(1)}, bf16[192,512]{1,0:T(8,128)(2,1)S(1)}, u32[]{:S(2)}, u32[]{:S(2)}) collective-permute-start(bf16[192,512]{1,0:T(8,128)(2,1)S(1)} %multiply_convert_fusion.5), channel_id=1, source_target_pairs={{0,32},{8,40},{16,48},{24,56},{32,64},{40,72},{48,80},{56,88},{64,... | collective-permute-start | bytes 589832 | tf_op jit(solution)/shard_map/ppermute | solution.py:12
  271.3 15.1 %collective-permute-start.6 = (bf16[192,512]{1,0:T(8,128)(2,1)S(1)}, bf16[192,512]{1,0:T(8,128)(2,1)S(1)}, u32[]{:S(2)}, u32[]{:S(2)}) collective-permute-start(bf16[192,512]{1,0:T(8,128)(2,1)S(1)} %multiply_convert_fusion.5), channel_id=1, source_target_pairs={{32,0},{40,8},{48,16},{56,24},{64,32},{72,40},{80,48},{88,56},{96,... | collective-permute-start | bytes 589832 | tf_op jit(solution)/shard_map/ppermute | solution.py:12
  (11 other events, 19.1 us)
Sparse Core Ops, SparseCore 0:
  10.1 61.5 all-gather.4
  74.3 49.3 all-gather.6
  138.6 70.7 all-gather.10
  211.9 49.9 all-gather.8
  267.2 562.9 all-reduce.2
where the time goes:
time: 843 us; the launch traced here: 842 us
  waiting for transfers between devices  737 us (87%)
  starting transfers between devices  51.4 us (6%)
  matrix products  17 us (2%)
  between operations  14.2 us (2%)
  local copies, waits for them, and re-layouts  13.1 us (2%)
  other arithmetic  9.59 us (1%)
    psum x1, waiting for transfers between devices, block_backward_step(): summed = lax.psum((conv_grad, point_grad), 'seq')  540 us
    all_gather x2, waiting for transfers between devices, block_forward_step(): gathered = lax.all_gather(activated, 'grp', axis=0, tiled=True)  89.4 us
    all_gather x2, waiting for transfers between devices, block_backward_step(): block_in = lax.all_gather(grad_out, 'grp', axis=0, tiled=True)  70.3 us
    ppermute x8, starting transfers between devices, passed_along(): return lax.ppermute(block, axis, route)  38.4 us
    ppermute x8, waiting for transfers between devices, passed_along(): return lax.ppermute(block, axis, route)  21.3 us
  transfers between devices with their start and end apart: 15, of which 12 were waited for; matrix products, arithmetic and copies ran while one was open for 3% of the time, Pallas kernels for 0%

commit v1 on v0

--- a/solution.py
+++ b/solution.py
@@ -70,7 +70,15 @@
         + group_apply(tap_set[2], tap_weights(conv_weight, 2))
     )
     activated = jax.nn.silu(hidden).astype(jnp.bfloat16)
-    gathered = lax.all_gather(activated, "grp", axis=0, tiled=True)
+    gathered = jnp.concatenate(
+        lax.all_to_all(
+            jnp.stack([activated for _ in range(lax.psum(1, "grp"))], axis=0),
+            "grp",
+            split_axis=0,
+            concat_axis=0,
+        ),
+        axis=0,
+    )
     return (tap_set, hidden, gathered)
 
 

time: 843 us -> 793 us (0.941)
  waiting for transfers between devices: 737 us -> 661 us
  starting transfers between devices: 51.4 us -> 67 us
    all_gather x2 -> x0, waiting for transfers between devices: 89.4 us -> none  [block_forward_step(): gathered = lax.all_gather(activated, 'grp', axis=0, tiled=True)]
    all_to_all x0 -> x2, starting transfers between devices: none -> 17 us  [block_forward_step(): lax.all_to_all(jnp.stack([activated for _ in range(lax.psum(1, 'grp'))],...]
    all_to_all x2, waiting for transfers between devices: 15.1 us -> 0.95 us  [block_backward_step(): lax.all_to_all(pointwise, 'grp', split_axis=1, concat_axis=0, tiled=True)]
    all_gather x2, waiting for transfers between devices: 70.3 us -> 83.5 us  [block_backward_step(): block_in = lax.all_gather(grad_out, 'grp', axis=0, tiled=True)]
    ppermute x8, waiting for transfers between devices: 21.3 us -> 33.7 us  [passed_along(): return lax.ppermute(block, axis, route)]
  transfers between devices with their start and end apart: 15 -> 15, of which waited for: 12 -> 9; matrix products, arithmetic and copies ran while one was open for 3% -> 4% of each run, Pallas kernels for 0% -> 0%
where the time goes in v1:
time: 793 us; the launch traced here: 791 us
  waiting for transfers between devices  661 us (83%)
  starting transfers between devices  67 us (8%)
  matrix products  19.5 us (2%)
  local copies, waits for them, and re-layouts  18.3 us (2%)
  between operations  14.2 us (2%)
  other arithmetic  11.4 us (1%)
    psum x1, waiting for transfers between devices, block_backward_step(): summed = lax.psum((conv_grad, point_grad), 'seq')  543 us
    all_gather x2, waiting for transfers between devices, block_backward_step(): block_in = lax.all_gather(grad_out, 'grp', axis=0, tiled=True)  83.5 us
    ppermute x8, starting transfers between devices, passed_along(): return lax.ppermute(block, axis, route)  36.6 us
    ppermute x8, waiting for transfers between devices, passed_along(): return lax.ppermute(block, axis, route)  33.7 us
    all_to_all x2, starting transfers between devices, block_forward_step(): lax.all_to_all(jnp.stack([activated for _ in range(lax.psum(1, 'grp'))],...  17 us
  transfers between devices with their start and end apart: 15, of which 9 were waited for; matrix products, arithmetic and copies ran while one was open for 4% of the time, Pallas kernels for 0%

profile of v1, /device:TPU:1, one launch (start us, length us, event | category | flops | bytes accessed | tf_op | source)
XLA Modules:
  0.0 791.5 jit_solution(9601181794721546733)
XLA Ops:
  7.2 2.3 copy.12
  9.5 6.6 all-to-all-start
  16.4 2.0 gather_fusion
  19.8 4.9 collective-permute-start
  26.5 3.1 collective-permute-done.1
  32.2 3.6 all-to-all-start.1
  35.8 2.2 reduce
  38.3 49.1 %all-gather.3.cloned.1.call-done = bf16[1536,512]{1,0:T(8,128)(2,1)} async-done(((bf16[192,512]{1,0:T(8,128)(2,1)}), bf16[1536,512]{1,0:T(8,128)(2,1)}) %all-gather.3.cloned.1.call-update) | async-done | bytes 1572880 | tf_op jit(solution)/shard_map/all_gather | solution.py:94
  87.3 2.0 convolution_convert_fusion.1
  92.2 13.6 %collective-permute-start.2 = (bf16[192,512]{1,0:T(8,128)(2,1)S(1)}, bf16[192,512]{1,0:T(8,128)(2,1)S(1)}, u32[]{:S(2)}, u32[]{:S(2)}) collective-permute-start(bf16[192,512]{1,0:T(8,128)(2,1)S(1)} %fusion.12), channel_id=1, source_target_pairs={{0,64},{8,72},{16,80},{24,88},{32,96},{40,104},{48,112},{56,120},{... | collective-permute-start | bytes 589832 | tf_op jit(solution)/shard_map/ppermute | solution.py:12
  110.6 13.4 %all-to-all-start.3 = ((bf16[8,192,512]{2,1,0:T(8,128)(2,1)}), bf16[8,192,512]{2,1,0:T(8,128)(2,1)S(1)}, u32[]{:S(2)}, u32[]{:S(2)}) async-start(bf16[8,192,512]{2,1,0:T(8,128)(2,1)} %stack.55), calls=%async_computation.3 | async-start | bytes 3145728 | tf_op jit(solution)/shard_map/all_to_all | solution.py:74
  124.0 8.8 %collective-permute-start.5 = (bf16[192,512]{1,0:T(8,128)(2,1)S(1)}, bf16[192,512]{1,0:T(8,128)(2,1)S(1)}, u32[]{:S(2)}, u32[]{:S(2)}) collective-permute-start(bf16[192,512]{1,0:T(8,128)(2,1)S(1)} %get-tuple-element.17), channel_id=1, source_target_pairs={{0,64},{8,72},{16,80},{24,88},{32,96},{40,104},{48,112},{56,120},{... | collective-permute-start | bytes 589832 | tf_op jit(solution)/shard_map/ppermute | solution.py:12
  135.2 13.6 %collective-permute-done.4 = bf16[192,512]{1,0:T(8,128)(2,1)S(1)} collective-permute-done((bf16[192,512]{1,0:T(8,128)(2,1)S(1)}, bf16[192,512]{1,0:T(8,128)(2,1)S(1)}, u32[]{:S(2)}, u32[]{:S(2)}) %collective-permute-start.4) | collective-permute-done | bytes 196640 | tf_op jit(solution)/shard_map/ppermute | solution.py:12
  151.8 2.3 copy.15
  154.1 6.5 all-to-all-start.2
  165.4 2.4 reshape.246
  172.1 34.4 %all-gather.5.cloned.1.call-done = bf16[1536,512]{1,0:T(8,128)(2,1)} async-done(((bf16[192,512]{1,0:T(8,128)(2,1)}), bf16[1536,512]{1,0:T(8,128)(2,1)}) %all-gather.5.cloned.1.call-update) | async-done | bytes 1572880 | tf_op jit(solution)/shard_map/all_gather | solution.py:94
  206.5 2.2 fusion
  212.0 4.2 collective-permute-start.7
  217.7 15.1 %collective-permute-done.6 = bf16[192,512]{1,0:T(8,128)(2,1)S(1)} collective-permute-done((bf16[192,512]{1,0:T(8,128)(2,1)S(1)}, bf16[192,512]{1,0:T(8,128)(2,1)S(1)}, u32[]{:S(2)}, u32[]{:S(2)}) %collective-permute-start.6) | collective-permute-done | bytes 196640 | tf_op jit(solution)/shard_map/ppermute | solution.py:12
  233.4 2.4 scatter_custom_fusion
  236.6 542.8 %all-reduce.3.cloned.1.call-done = (f32[1,110592]{1,0:T(1,128)}, f32[192,1536]{1,0:T(8,128)}, f32[1,110592]{1,0:T(1,128)}, f32[192,1536]{1,0:T(8,128)}) async-done(((f32[1,110592]{1,0:T(1,128)}, f32[192,1536]{1,0:T(8,128)}, f32[1,110592]{1,0:T(1,128)}, f32[192,1536]{1,0:T(8,128)}), (f32[1,110592]{1,0:T(1,128)}, f32[192,1536]{1,0:T(8,128)}, f32[1,110592]{1,0:T(1,128)}, ...) | async-done | bytes 3244048 | tf_op jit(solution)/shard_map/psum | solution.py:117
  779.4 3.1 multiply_convert_fusion.2
  782.5 2.5 multiply_convert_fusion
  (98 shorter events, 34.3 us)
Async XLA Ops:
  7.2 9.0 %copy-start.19 = (s32[512]{0:T(512)S(1)}, s32[512]{0:T(512)}, u32[]{:S(2)}) copy-start(s32[512]{0:T(512)} %param.8) | copy-start | bytes 6148
  7.2 9.0 %copy-start.15 = (bf16[192,512]{1,0:T(8,128)(2,1)S(1)}, bf16[192,512]{1,0:T(8,128)(2,1)}, u32[]{:S(2)}) copy-start(bf16[192,512]{1,0:T(8,128)(2,1)} %param.7) | copy-start | bytes 589828
  9.5 21.5 %all-to-all-start = ((bf16[192,8,192]{0,2,1:T(8,128)(2,1)}), bf16[192,8,192]{0,2,1:T(8,128)(2,1)S(1)}, u32[]{:S(2)}, u32[]{:S(2)}) async-start(bf16[192,8,192]{0,2,1:T(8,128)(2,1)} %bitcast), calls=%async_computation | async-start | bytes 1572864 | tf_op jit(solution)/shard_map/all_to_all | solution.py:93
  16.1 71.2 %all-gather.3.cloned.1.call-start = ((), (), s32[]{:S(2)}) async-start(), calls=%async_computation.4 | async-start | bytes 1769472 | tf_op jit(solution)/shard_map/all_gather | solution.py:94
  16.2 8.5 %copy-start.12 = (bf16[1,110592]{1,0:T(2,128)(2,1)S(1)}, bf16[1,110592]{1,0:T(2,128)(2,1)}, u32[]{:S(2)}) copy-start(bf16[1,110592]{1,0:T(2,128)(2,1)} %param.10) | copy-start | bytes 663556
  18.5 11.1 %collective-permute-start.1 = (bf16[192,512]{1,0:T(8,128)(2,1)S(1)}, bf16[192,512]{1,0:T(8,128)(2,1)S(1)}, u32[]{:S(2)}, u32[]{:S(2)}) collective-permute-start(bf16[192,512]{1,0:T(8,128)(2,1)S(1)} %fusion.17), channel_id=1, source_target_pairs={{32,0},{40,8},{48,16},{56,24},{64,32},{72,40},{80,48},{88,56},{96,... | collective-permute-start | bytes 589832 | tf_op jit(solution)/shard_map/ppermute | solution.py:12
  19.8 10.1 %collective-permute-start = (bf16[192,512]{1,0:T(8,128)(2,1)S(1)}, bf16[192,512]{1,0:T(8,128)(2,1)S(1)}, u32[]{:S(2)}, u32[]{:S(2)}) collective-permute-start(bf16[192,512]{1,0:T(8,128)(2,1)S(1)} %fusion.17), channel_id=1, source_target_pairs={{0,32},{8,40},{16,48},{24,56},{32,64},{40,72},{48,80},{56,88},{64,... | collective-permute-start | bytes 589832 | tf_op jit(solution)/shard_map/ppermute | solution.py:12
  32.2 58.1 %all-to-all-start.1 = ((bf16[8,192,512]{2,1,0:T(8,128)(2,1)}), bf16[8,192,512]{2,1,0:T(8,128)(2,1)S(1)}, u32[]{:S(2)}, u32[]{:S(2)}) async-start(bf16[8,192,512]{2,1,0:T(8,128)(2,1)} %stack.20), calls=%async_computation.1 | async-start | bytes 3145728 | tf_op jit(solution)/shard_map/all_to_all | solution.py:74
  38.2 70.4 %copy-start.5 = (bf16[1,3,192,192]{3,2,1,0:T(8,128)(2,1)}, bf16[1,3,192,192]{3,2,1,0:T(8,128)(2,1)S(1)}, u32[]{:S(2)}) copy-start(bf16[1,3,192,192]{3,2,1,0:T(8,128)(2,1)S(1)} %reshape.240) | copy-start | bytes 663556
  90.4 18.2 %copy-start.14 = (f32[192,512]{1,0:T(8,128)S(1)}, f32[192,512]{1,0:T(8,128)}, u32[]{:S(2)}) copy-start(f32[192,512]{1,0:T(8,128)} %convert_reduce_fusion.1) | copy-start | bytes 1179652
  90.8 18.2 %copy-start.7 = (bf16[192,512]{1,0:T(8,128)(2,1)}, bf16[192,512]{1,0:T(8,128)(2,1)S(1)}, u32[]{:S(2)}) copy-start(bf16[192,512]{1,0:T(8,128)(2,1)S(1)} %fusion.12) | copy-start | bytes 589828
  90.9 17.0 %collective-permute-start.3 = (bf16[192,512]{1,0:T(8,128)(2,1)S(1)}, bf16[192,512]{1,0:T(8,128)(2,1)S(1)}, u32[]{:S(2)}, u32[]{:S(2)}) collective-permute-start(bf16[192,512]{1,0:T(8,128)(2,1)S(1)} %fusion.12), channel_id=1, source_target_pairs={{64,0},{72,8},{80,16},{88,24},{96,32},{104,40},{112,48},{120,56},{... | collective-permute-start | bytes 589832 | tf_op jit(solution)/shard_map/ppermute | solution.py:12
  92.2 16.4 %collective-permute-start.2 = (bf16[192,512]{1,0:T(8,128)(2,1)S(1)}, bf16[192,512]{1,0:T(8,128)(2,1)S(1)}, u32[]{:S(2)}, u32[]{:S(2)}) collective-permute-start(bf16[192,512]{1,0:T(8,128)(2,1)S(1)} %fusion.12), channel_id=1, source_target_pairs={{0,64},{8,72},{16,80},{24,88},{32,96},{40,104},{48,112},{56,120},{... | collective-permute-start | bytes 589832 | tf_op jit(solution)/shard_map/ppermute | solution.py:12
  109.3 51.5 %copy-start.1 = (bf16[192,512]{1,0:T(8,128)(2,1)}, bf16[192,512]{1,0:T(8,128)(2,1)S(1)}, u32[]{:S(2)}) copy-start(bf16[192,512]{1,0:T(8,128)(2,1)S(1)} %get-tuple-element.17) | copy-start | bytes 589828
  110.6 43.5 %all-to-all-start.3 = ((bf16[8,192,512]{2,1,0:T(8,128)(2,1)}), bf16[8,192,512]{2,1,0:T(8,128)(2,1)S(1)}, u32[]{:S(2)}, u32[]{:S(2)}) async-start(bf16[8,192,512]{2,1,0:T(8,128)(2,1)} %stack.55), calls=%async_computation.3 | async-start | bytes 3145728 | tf_op jit(solution)/shard_map/all_to_all | solution.py:74
  124.0 82.5 %all-gather.5.cloned.1.call-start = ((), (), s32[]{:S(2)}) async-start(), calls=%async_computation.5 | async-start | bytes 1769472 | tf_op jit(solution)/shard_map/all_gather | solution.py:94
  124.0 26.0 %collective-permute-start.5 = (bf16[192,512]{1,0:T(8,128)(2,1)S(1)}, bf16[192,512]{1,0:T(8,128)(2,1)S(1)}, u32[]{:S(2)}, u32[]{:S(2)}) collective-permute-start(bf16[192,512]{1,0:T(8,128)(2,1)S(1)} %get-tuple-element.17), channel_id=1, source_target_pairs={{0,64},{8,72},{16,80},{24,88},{32,96},{40,104},{48,112},{56,120},{... | collective-permute-start | bytes 589832 | tf_op jit(solution)/shard_map/ppermute | solution.py:12
  132.8 16.0 %collective-permute-start.4 = (bf16[192,512]{1,0:T(8,128)(2,1)S(1)}, bf16[192,512]{1,0:T(8,128)(2,1)S(1)}, u32[]{:S(2)}, u32[]{:S(2)}) collective-permute-start(bf16[192,512]{1,0:T(8,128)(2,1)S(1)} %get-tuple-element.17), channel_id=1, source_target_pairs={{64,0},{72,8},{80,16},{88,24},{96,32},{104,40},{112,48},{120,56},{... | collective-permute-start | bytes 589832 | tf_op jit(solution)/shard_map/ppermute | solution.py:12
  154.1 18.0 %all-to-all-start.2 = ((bf16[192,8,192]{0,2,1:T(8,128)(2,1)}), bf16[192,8,192]{0,2,1:T(8,128)(2,1)}, u32[]{:S(2)}, u32[]{:S(2)}) async-start(bf16[192,8,192]{0,2,1:T(8,128)(2,1)} %bitcast.134), calls=%async_computation.2 | async-start | bytes 1572864 | tf_op jit(solution)/shard_map/all_to_all | solution.py:93
  160.5 618.9 %all-reduce.3.cloned.1.call-start = ((), (), s32[]{:S(2)}) async-start(), calls=%async_computation.6 | async-start | bytes 6488064 | tf_op jit(solution)/shard_map/psum | solution.py:117
  161.9 5.8 copy-start
  212.0 5.5 copy-start.4
  212.0 21.0 %collective-permute-start.7 = (bf16[192,512]{1,0:T(8,128)(2,1)S(1)}, bf16[192,512]{1,0:T(8,128)(2,1)S(1)}, u32[]{:S(2)}, u32[]{:S(2)}) collective-permute-start(bf16[192,512]{1,0:T(8,128)(2,1)S(1)} %multiply_convert_fusion.5), channel_id=1, source_target_pairs={{0,32},{8,40},{16,48},{24,56},{32,64},{40,72},{48,80},{56,88},{64,... | collective-permute-start | bytes 589832 | tf_op jit(solution)/shard_map/ppermute | solution.py:12
  216.2 16.6 %collective-permute-start.6 = (bf16[192,512]{1,0:T(8,128)(2,1)S(1)}, bf16[192,512]{1,0:T(8,128)(2,1)S(1)}, u32[]{:S(2)}, u32[]{:S(2)}) collective-permute-start(bf16[192,512]{1,0:T(8,128)(2,1)S(1)} %multiply_convert_fusion.5), channel_id=1, source_target_pairs={{32,0},{40,8},{48,16},{56,24},{64,32},{72,40},{80,48},{88,56},{96,... | collective-permute-start | bytes 589832 | tf_op jit(solution)/shard_map/ppermute | solution.py:12
  (11 other events, 20.6 us)
Sparse Core Ops, SparseCore 0:
  24.8 62.4 all-gather.2
  151.9 54.5 all-gather.4
  212.1 567.2 all-reduce.2
